TPU v7x, 32 devices: a whole 2x2x4 slice. The times are simulated.
32 devices in a mesh: gen: 4 (over y, x), fit: 8 (over z, core).
Axes of the slice: x: 2, y: 2, z: 4, core: 2. Of those that a mesh axis runs over, the one named last changes fastest.
Arguments:
- raw_columns: bfloat16 [8, 2000, 2000], P(None, 'gen', 'fit'), as said below
- pivot_pairs: int32 [8], replicated, may hold values from 0 to 3999999, as said below
- collocation: bfloat16 [2000, 4096], P('gen', 'fit'), may hold values from -0.125 to 0.125
- metric_factor: float32 [4096, 4096], P('fit', 'gen'), as said below
Outputs:
- panel: float32 [8, 4096], P('gen', 'fit')
Inputs may be any that keep to these rules, and one draw needn't show every extreme that they name: `pivot_pairs`: 8 distinct orbital-pair indices p * 2000 + q. The entries at the pivots, raw_columns[P, pivot_pairs[Q] // 2000, pivot_pairs[Q] % 2000], form a symmetric positive definite matrix. `metric_factor`: lower triangular with a positive diagonal.
All inputs are finite; a program needn't handle non-finite values.
Results may differ from a plain program's by a relative error of at most 0.0029.
Values may be sent and summed in bfloat16 or wider, within the bound.
No kernel may reach another device: no remote copies, remote signals or barrier semaphores. Data moves between devices by JAX's collectives and lax.ppermute only.
A program may use at most 64 MiB of HBM per device.

v0:
```python
import math
import jax
import jax.numpy as jnp
from jax import lax
from jax.sharding import PartitionSpec as P

NORB = 2000


def spread(value, axis, source):
    kept = jnp.where(lax.axis_index(axis) == source, value, 0).astype(value.dtype)
    return lax.psum(kept, axis)


def project_block(vectors, stacked, orbital_count):
    point_count = stacked.shape[1]
    block_width = math.gcd(point_count, 512)
    block_count = point_count // block_width
    pair_count = stacked.shape[0] - orbital_count
    orbital_part = (
        stacked[:orbital_count].reshape(orbital_count, block_count, block_width).transpose(1, 0, 2)
    )
    pair_part = (
        stacked[orbital_count:].reshape(pair_count, block_count, block_width).transpose(1, 0, 2)
    )

    def one_block(pieces):
        mixed_terms = jnp.einsum(
            "apq,pn->aqn", vectors, pieces[0], preferred_element_type=jnp.float32
        )
        return jnp.sum(mixed_terms * pieces[1].astype(jnp.float32)[None], axis=1)

    blocks = lax.map(one_block, (orbital_part, pair_part))
    return blocks.transpose(1, 0, 2).reshape(vectors.shape[0], point_count)


def on_device(raw_columns, pivot_pairs, collocation, metric_factor):
    vec_total, orb_block, pair_block = raw_columns.shape
    gen_count = lax.axis_size("gen")
    fit_count = lax.axis_size("fit")
    gen_index = lax.axis_index("gen")
    fit_index = lax.axis_index("fit")
    point_dev = metric_factor.shape[0]
    vec_dev = vec_total // gen_count
    pair_first = pivot_pairs // NORB
    pair_second = pivot_pairs % NORB
    row_hits = (
        pair_first[:, None] == gen_index * orb_block + jnp.arange(orb_block)[None, :]
    ).astype(jnp.bfloat16)
    col_hits = (
        pair_second[:, None] == fit_index * pair_block + jnp.arange(pair_block)[None, :]
    ).astype(jnp.float32)
    picked = jnp.einsum("apq,bp->abq", raw_columns, row_hits, preferred_element_type=jnp.float32)
    own_entries = jnp.sum(picked * col_hits[None], axis=2)
    pivot_block = lax.psum(own_entries, ("gen", "fit"))
    factor = jnp.linalg.cholesky(pivot_block)
    flat_columns = raw_columns.reshape(vec_total, orb_block * pair_block).astype(jnp.float32)
    vectors = jax.scipy.linalg.solve_triangular(factor, flat_columns, lower=True)
    vectors = vectors.astype(jnp.bfloat16).reshape(vec_total, orb_block, pair_block)
    group_ratio = fit_count // gen_count
    owner_index = fit_index // group_ratio
    portion = fit_index % group_ratio
    orbital_side = lax.all_gather(collocation, "fit", axis=1, tiled=True)
    wide_slice = lax.dynamic_slice_in_dim(orbital_side, portion * pair_block, pair_block, 0)
    pair_side = spread(wide_slice, "gen", owner_index)
    partial_panel = project_block(
        vectors, jnp.concatenate([orbital_side, pair_side], axis=0), orb_block
    )
    arranged = partial_panel.reshape(gen_count, vec_dev, fit_count, point_dev).transpose(0, 2, 1, 3)
    arranged = arranged.reshape(gen_count * fit_count * vec_dev, point_dev)
    summed = lax.psum_scatter(arranged, ("gen", "fit"), scatter_dimension=0, tiled=True)
    remaining_start = jnp.zeros((vec_total, point_dev), jnp.float32)
    remaining_start = lax.dynamic_update_slice_in_dim(
        remaining_start, summed, gen_index * vec_dev, 0
    )

    def advance(turn_index, carried):
        remaining, solved = carried
        turn_owner = turn_index // group_ratio
        local_start = turn_index % group_ratio * point_dev
        whole_rest = lax.psum(remaining, "gen")
        column_part = lax.dynamic_slice_in_dim(metric_factor, local_start, point_dev, 1)
        candidate = jax.scipy.linalg.solve_triangular(column_part, whole_rest.T, lower=True).T
        holder = jnp.logical_and(fit_index == turn_index, gen_index == turn_owner)
        candidate = jnp.where(holder, candidate, 0.0)
        arrived = spread(candidate, ("gen", "fit"), turn_owner * fit_count + turn_index)
        update = jnp.dot(arrived, column_part.T, precision=lax.Precision.HIGHEST)
        remaining = remaining - jnp.where(gen_index == turn_owner, update, 0.0)
        own_rows = lax.dynamic_slice_in_dim(arrived, gen_index * vec_dev, vec_dev, 0)
        solved = jnp.where(fit_index == turn_index, own_rows, solved)
        return (remaining, solved)

    initial = jnp.zeros((vec_dev, point_dev), jnp.float32)
    remaining, solved = lax.fori_loop(0, fit_count, advance, (remaining_start, initial))
    return solved


def solution(mesh):
    in_specs = (P(None, "gen", "fit"), P(), P("gen", "fit"), P("fit", "gen"))
    out_specs = P("gen", "fit")
    return jax.shard_map(
        on_device, mesh=mesh, in_specs=in_specs, out_specs=out_specs, check_vma=False
    )
```

profile of v0, /device:TPU:0, one launch (start us, length us, event | category | flops | bytes accessed | tf_op | source)
XLA Modules:
  0.0 1175.4 jit_solution(14042528507513244858)
XLA Ops:
  7.3 50.9 %all-gather.2.cloned.1.call-done = bf16[500,4096]{1,0:T(8,128)(2,1)} async-done(((bf16[500,512]{1,0:T(8,128)(2,1)}), bf16[500,4096]{1,0:T(8,128)(2,1)}) %all-gather.2.cloned.1.call-update) | async-done | bytes 4096016 | tf_op jit(solution)/shard_map/all_gather | solution.py:63
  67.0 39.1 %psum.42 = f32[8,8]{0,1:T(8,128)S(1)} all-reduce(f32[8,8]{0,1:T(8,128)S(1)} %bitcast.108), channel_id=1, replica_groups=mesh['gen'=4,'fit'=8] {'gen','fit'}, use_global_device_ids=true, to_apply=%region_2.3 | all-reduce | flops 64 | bytes 512 | tf_op jit(solution)/shard_map/psum | solution.py:55
  146.3 35.0 %while.31 = (s32[]{:T(128)}, f32[8,8,512]{2,1,0:T(8,128)S(1)}, bf16[8,500,512]{2,1,0:T(8,128)(2,1)}, bf16[8,500,250]{2,1,0:T(8,128)(2,1)}, bf16[8,250,512]{1,2,0:T(8,128)(2,1)}, /*index=5*/s32[]{:T(128)}) while((s32[]{:T(128)}, f32[8,8,512]{2,1,0:T(8,128)S(1)}, bf16[8,500,512]{2,1,0:T(8,128)(2,1)}, bf16[8,500,250]{2,1,0:T(8,128)(2,1)}, ...), condition=%wide.region_7.8_spmd, body=%wide.region_5.7_spmd.sunk | while | flops 1026171904 | bytes 4934221 | solution.py:33
  182.1 122.3 %all-reduce.6.cloned.1.call-done = f32[64,512]{1,0:T(8,128)} async-done(((f32[64,512]{1,0:T(8,128)}), f32[64,512]{1,0:T(8,128)}) %all-reduce.6.cloned.1.call-update) | async-done | bytes 131088
  305.2 863.1 %while.33 = (s32[]{:T(128)}, f32[8,512]{1,0:T(8,128)S(1)}, f32[2,512]{1,0:T(2,128)S(1)}, s32[]{:T(128)}, s32[]{:T(128)}, /*index=5*/f32[512,1024]{1,0:T(8,128)S(...) while((s32[]{:T(128)}, f32[8,512]{1,0:T(8,128)S(1)}, ...), condition=%wide.region_12.13_spmd.clone, body=%wide.region_9.12_spmd.clone.sunk | while | flops 41468964 | bytes 4176043 | solution.py:94
  315.6 40.1 %custom-call.26 = f32[4,128,128]{1,2,0:T(8,128)S(1)} custom-call(f32[4,128,128]{2,1,0:T(8,128)} %get-tuple-element.386), custom_call_target="InvertDiagBlocksLowerTriangular" | custom-call | tf_op jit(solution)/shard_map/while/body/eval_jaxpr/jit(_solve_triangular)/triangular_solve | solution.py:83
  373.1 38.4 %psum.49 = f32[8,512]{1,0:T(8,128)S(1)} all-reduce(f32[8,512]{1,0:T(8,128)S(1)} %fusion.88), channel_id=1, replica_groups=mesh['gen'=4,'fit'=8] {'gen','fit'}, use_global_device_ids=true, to_apply=%region_11.11 | all-reduce | flops 4096 | bytes 32768 | tf_op jit(solution)/shard_map/while/body/eval_jaxpr/psum | solution.py:12
  422.8 40.1 %custom-call.26 = f32[4,128,128]{1,2,0:T(8,128)S(1)} custom-call(f32[4,128,128]{2,1,0:T(8,128)} %get-tuple-element.386), custom_call_target="InvertDiagBlocksLowerTriangular" | custom-call | tf_op jit(solution)/shard_map/while/body/eval_jaxpr/jit(_solve_triangular)/triangular_solve | solution.py:83
  481.1 38.4 %psum.49 = f32[8,512]{1,0:T(8,128)S(1)} all-reduce(f32[8,512]{1,0:T(8,128)S(1)} %fusion.88), channel_id=1, replica_groups=mesh['gen'=4,'fit'=8] {'gen','fit'}, use_global_device_ids=true, to_apply=%region_11.11 | all-reduce | flops 4096 | bytes 32768 | tf_op jit(solution)/shard_map/while/body/eval_jaxpr/psum | solution.py:12
  530.7 40.1 %custom-call.26 = f32[4,128,128]{1,2,0:T(8,128)S(1)} custom-call(f32[4,128,128]{2,1,0:T(8,128)} %get-tuple-element.386), custom_call_target="InvertDiagBlocksLowerTriangular" | custom-call | tf_op jit(solution)/shard_map/while/body/eval_jaxpr/jit(_solve_triangular)/triangular_solve | solution.py:83
  589.1 38.4 %psum.49 = f32[8,512]{1,0:T(8,128)S(1)} all-reduce(f32[8,512]{1,0:T(8,128)S(1)} %fusion.88), channel_id=1, replica_groups=mesh['gen'=4,'fit'=8] {'gen','fit'}, use_global_device_ids=true, to_apply=%region_11.11 | all-reduce | flops 4096 | bytes 32768 | tf_op jit(solution)/shard_map/while/body/eval_jaxpr/psum | solution.py:12
  638.7 40.1 %custom-call.26 = f32[4,128,128]{1,2,0:T(8,128)S(1)} custom-call(f32[4,128,128]{2,1,0:T(8,128)} %get-tuple-element.386), custom_call_target="InvertDiagBlocksLowerTriangular" | custom-call | tf_op jit(solution)/shard_map/while/body/eval_jaxpr/jit(_solve_triangular)/triangular_solve | solution.py:83
  697.0 38.4 %psum.49 = f32[8,512]{1,0:T(8,128)S(1)} all-reduce(f32[8,512]{1,0:T(8,128)S(1)} %fusion.88), channel_id=1, replica_groups=mesh['gen'=4,'fit'=8] {'gen','fit'}, use_global_device_ids=true, to_apply=%region_11.11 | all-reduce | flops 4096 | bytes 32768 | tf_op jit(solution)/shard_map/while/body/eval_jaxpr/psum | solution.py:12
  746.7 40.1 %custom-call.26 = f32[4,128,128]{1,2,0:T(8,128)S(1)} custom-call(f32[4,128,128]{2,1,0:T(8,128)} %get-tuple-element.386), custom_call_target="InvertDiagBlocksLowerTriangular" | custom-call | tf_op jit(solution)/shard_map/while/body/eval_jaxpr/jit(_solve_triangular)/triangular_solve | solution.py:83
  805.0 38.4 %psum.49 = f32[8,512]{1,0:T(8,128)S(1)} all-reduce(f32[8,512]{1,0:T(8,128)S(1)} %fusion.88), channel_id=1, replica_groups=mesh['gen'=4,'fit'=8] {'gen','fit'}, use_global_device_ids=true, to_apply=%region_11.11 | all-reduce | flops 4096 | bytes 32768 | tf_op jit(solution)/shard_map/while/body/eval_jaxpr/psum | solution.py:12
  854.6 40.1 %custom-call.26 = f32[4,128,128]{1,2,0:T(8,128)S(1)} custom-call(f32[4,128,128]{2,1,0:T(8,128)} %get-tuple-element.386), custom_call_target="InvertDiagBlocksLowerTriangular" | custom-call | tf_op jit(solution)/shard_map/while/body/eval_jaxpr/jit(_solve_triangular)/triangular_solve | solution.py:83
  894.8 16.8 %psum.48 = f32[512,8]{0,1:T(8,128)S(1)} all-reduce(f32[512,8]{0,1:T(8,128)S(1)} %bitcast.105), channel_id=1, replica_groups=mesh['gen'=4,'fit'=8] {'gen'}, use_global_device_ids=true, to_apply=%region_10.10 | all-reduce | flops 4096 | bytes 32768 | tf_op jit(solution)/shard_map/while/body/eval_jaxpr/psum | solution.py:81
  913.0 38.4 %psum.49 = f32[8,512]{1,0:T(8,128)S(1)} all-reduce(f32[8,512]{1,0:T(8,128)S(1)} %fusion.88), channel_id=1, replica_groups=mesh['gen'=4,'fit'=8] {'gen','fit'}, use_global_device_ids=true, to_apply=%region_11.11 | all-reduce | flops 4096 | bytes 32768 | tf_op jit(solution)/shard_map/while/body/eval_jaxpr/psum | solution.py:12
  962.6 40.1 %custom-call.26 = f32[4,128,128]{1,2,0:T(8,128)S(1)} custom-call(f32[4,128,128]{2,1,0:T(8,128)} %get-tuple-element.386), custom_call_target="InvertDiagBlocksLowerTriangular" | custom-call | tf_op jit(solution)/shard_map/while/body/eval_jaxpr/jit(_solve_triangular)/triangular_solve | solution.py:83
  1002.7 16.8 %psum.48 = f32[512,8]{0,1:T(8,128)S(1)} all-reduce(f32[512,8]{0,1:T(8,128)S(1)} %bitcast.105), channel_id=1, replica_groups=mesh['gen'=4,'fit'=8] {'gen'}, use_global_device_ids=true, to_apply=%region_10.10 | all-reduce | flops 4096 | bytes 32768 | tf_op jit(solution)/shard_map/while/body/eval_jaxpr/psum | solution.py:81
  1020.9 38.4 %psum.49 = f32[8,512]{1,0:T(8,128)S(1)} all-reduce(f32[8,512]{1,0:T(8,128)S(1)} %fusion.88), channel_id=1, replica_groups=mesh['gen'=4,'fit'=8] {'gen','fit'}, use_global_device_ids=true, to_apply=%region_11.11 | all-reduce | flops 4096 | bytes 32768 | tf_op jit(solution)/shard_map/while/body/eval_jaxpr/psum | solution.py:12
  1070.6 40.1 %custom-call.26 = f32[4,128,128]{1,2,0:T(8,128)S(1)} custom-call(f32[4,128,128]{2,1,0:T(8,128)} %get-tuple-element.386), custom_call_target="InvertDiagBlocksLowerTriangular" | custom-call | tf_op jit(solution)/shard_map/while/body/eval_jaxpr/jit(_solve_triangular)/triangular_solve | solution.py:83
  1110.7 16.8 %psum.48 = f32[512,8]{0,1:T(8,128)S(1)} all-reduce(f32[512,8]{0,1:T(8,128)S(1)} %bitcast.105), channel_id=1, replica_groups=mesh['gen'=4,'fit'=8] {'gen'}, use_global_device_ids=true, to_apply=%region_10.10 | all-reduce | flops 4096 | bytes 32768 | tf_op jit(solution)/shard_map/while/body/eval_jaxpr/psum | solution.py:81
  1128.9 38.4 %psum.49 = f32[8,512]{1,0:T(8,128)S(1)} all-reduce(f32[8,512]{1,0:T(8,128)S(1)} %fusion.88), channel_id=1, replica_groups=mesh['gen'=4,'fit'=8] {'gen','fit'}, use_global_device_ids=true, to_apply=%region_11.11 | all-reduce | flops 4096 | bytes 32768 | tf_op jit(solution)/shard_map/while/body/eval_jaxpr/psum | solution.py:12
  (306 shorter events, 350.3 us)
Async XLA Ops:
  6.5 51.7 %all-gather.2.cloned.1.call-start = ((), (), s32[]{:S(2)}) async-start(), calls=%async_computation | async-start | bytes 4644864 | tf_op jit(solution)/shard_map/all_gather | solution.py:63
  7.3 139.0 %all-reduce.4.cloned.1.call-start = ((), (), s32[]{:S(2)}) async-start(), calls=%async_computation.1 | async-start | bytes 4194304 | tf_op jit(solution)/shard_map/psum | solution.py:12
  62.9 1.6 copy-start.1
  63.0 3.3 copy-start.3
  63.0 241.5 %all-reduce.6.cloned.1.call-start = ((), (), s32[]{:S(2)}) async-start(), calls=%async_computation.2 | async-start | bytes 262144
  146.3 158.9 %copy-start = (f32[512,1024]{1,0:T(8,128)S(1)}, f32[512,1024]{1,0:T(8,128)}, u32[]{:S(2)}) copy-start(f32[512,1024]{1,0:T(8,128)} %param.11) | copy-start | bytes 6291460
  1168.3 0.6 copy-start.2
Sparse Core Ops, SparseCore 0:
  9.0 49.1 all-gather.1
  63.1 69.2 all-reduce.3
  182.2 122.1 all-reduce.5
where the time goes:
time: 1180 us
  blocking collectives  480 us (41%)
  other arithmetic  328 us (28%)
  waiting for transfers between devices  174 us (15%)
  local copies, waits for them, and re-layouts  132 us (11%)
  matrix products  47.8 us (4%)
  between operations  13.3 us (1%)
    another operation x24, other arithmetic, advance(): jax.scipy.linalg.solve_triangular(column_part, whole_rest.T, lower=True)  322 us
    psum x8, blocking collectives, spread(): return lax.psum(kept, axis)  307 us
    psum x8, blocking collectives, advance(): whole_rest = lax.psum(remaining, 'gen')  133 us
    unnamed x4, waiting for transfers between devices  123 us
    another operation x96, local copies, waits for them, and re-layouts  80.2 us
    all_gather x1, waiting for transfers between devices, on_device(): orbital_side = lax.all_gather(collocation, 'fit', axis=1, tiled=True)  50.9 us
    psum x1, blocking collectives, on_device(): pivot_block = lax.psum(own_entries, ('gen', 'fit'))  39.1 us
    dot_general x8, matrix products, one_block(): jnp.einsum('apq,pn->aqn', vectors, pieces[0], preferred_element_type=jnp....  25.1 us
  transfers between devices with their start and end apart: 3, of which 2 were waited for; matrix products, arithmetic and copies ran while one was open for 4% of the time, Pallas kernels for 0%

commit v1 on v0

--- a/solution.py
+++ b/solution.py
@@ -60,7 +60,12 @@
     group_ratio = fit_count // gen_count
     owner_index = fit_index // group_ratio
     portion = fit_index % group_ratio
-    orbital_side = lax.all_gather(collocation, "fit", axis=1, tiled=True)
+    ring = [collocation]
+    for hop in range(7):
+        ring.append(lax.ppermute(ring[-1], "fit", [(dev, (dev + 1) % 8) for dev in range(8)]))
+    orbital_side = jnp.roll(
+        jnp.concatenate(ring[::-1], axis=1), (lax.axis_index("fit") + 1) * ring[0].shape[1], axis=1
+    )
     wide_slice = lax.dynamic_slice_in_dim(orbital_side, portion * pair_block, pair_block, 0)
     pair_side = spread(wide_slice, "gen", owner_index)
     partial_panel = project_block(

time: 1180 us -> 1210 us (1.025)
  waiting for transfers between devices: 174 us -> 196 us
    ppermute x0 -> x7, waiting for transfers between devices: none -> 72.7 us  [on_device(): lax.ppermute(ring[-1], 'fit', [(dev, (dev + 1) % 8) for dev in range(8)])]
    all_gather x1 -> x0, waiting for transfers between devices: 50.9 us -> none  [on_device(): orbital_side = lax.all_gather(collocation, 'fit', axis=1, tiled=True)]
    unnamed x4 -> x3, waiting for transfers between devices: 123 us -> 123 us
  transfers between devices with their start and end apart: 3 -> 9, of which waited for: 2 -> 8; matrix products, arithmetic and copies ran while one was open for 4% -> 4% of each run, Pallas kernels for 0% -> 0%
where the time goes in v1:
time: 1210 us
  blocking collectives  479 us (40%)
  other arithmetic  327 us (27%)
  waiting for transfers between devices  196 us (16%)
  local copies, waits for them, and re-layouts  143 us (12%)
  matrix products  49.3 us (4%)
  between operations  13.7 us (1%)
    another operation x24, other arithmetic, advance(): jax.scipy.linalg.solve_triangular(column_part, whole_rest.T, lower=True)  322 us
    psum x8, blocking collectives, spread(): return lax.psum(kept, axis)  307 us
    psum x8, blocking collectives, advance(): whole_rest = lax.psum(remaining, 'gen')  133 us
    unnamed x3, waiting for transfers between devices  123 us
    another operation x96, local copies, waits for them, and re-layouts  80.2 us
    ppermute x7, waiting for transfers between devices, on_device(): lax.ppermute(ring[-1], 'fit', [(dev, (dev + 1) % 8) for dev in range(8)])  72.7 us
    psum x1, blocking collectives, on_device(): pivot_block = lax.psum(own_entries, ('gen', 'fit'))  38.6 us
    dot_general x8, matrix products, one_block(): jnp.einsum('apq,pn->aqn', vectors, pieces[0], preferred_element_type=jnp....  25.1 us
  transfers between devices with their start and end apart: 9, of which 8 were waited for; matrix products, arithmetic and copies ran while one was open for 4% of the time, Pallas kernels for 0%

profile of v1, /device:TPU:0, one launch (start us, length us, event | category | flops | bytes accessed | tf_op | source)
XLA Modules:
  0.0 1210.1 jit_solution(4453519686493123997)
XLA Ops:
  97.7 38.6 %psum.42 = f32[8,8]{0,1:T(8,128)S(1)} all-reduce(f32[8,8]{0,1:T(8,128)S(1)} %bitcast.108), channel_id=1, replica_groups=mesh['gen'=4,'fit'=8] {'gen','fit'}, use_global_device_ids=true, to_apply=%region_2.3 | all-reduce | flops 64 | bytes 512 | tf_op jit(solution)/shard_map/psum | solution.py:55
  179.7 35.0 %while.31 = (s32[]{:T(128)}, f32[8,8,512]{2,1,0:T(8,128)S(1)}, bf16[8,500,512]{2,1,0:T(8,128)(2,1)}, bf16[8,500,250]{2,1,0:T(8,128)(2,1)}, bf16[8,250,512]{1,2,0:T(8,128)(2,1)}, /*index=5*/s32[]{:T(128)}) while((s32[]{:T(128)}, f32[8,8,512]{2,1,0:T(8,128)S(1)}, bf16[8,500,512]{2,1,0:T(8,128)(2,1)}, bf16[8,500,250]{2,1,0:T(8,128)(2,1)}, ...), condition=%wide.region_7.8_spmd, body=%wide.region_5.7_spmd.sunk | while | flops 1026171904 | bytes 4934221 | solution.py:33
  215.6 123.2 %all-reduce.6.cloned.1.call-done = f32[64,512]{1,0:T(8,128)} async-done(((f32[64,512]{1,0:T(8,128)}), f32[64,512]{1,0:T(8,128)}) %all-reduce.6.cloned.1.call-update) | async-done | bytes 131088
  339.5 863.1 %while.33 = (s32[]{:T(128)}, f32[8,512]{1,0:T(8,128)S(1)}, f32[2,512]{1,0:T(2,128)S(1)}, s32[]{:T(128)}, s32[]{:T(128)}, /*index=5*/f32[512,1024]{1,0:T(8,128)S(...) while((s32[]{:T(128)}, f32[8,512]{1,0:T(8,128)S(1)}, ...), condition=%wide.region_12.13_spmd.clone, body=%wide.region_9.12_spmd.clone.sunk | while | flops 41468964 | bytes 4176043 | solution.py:99
  350.0 40.1 %custom-call.28 = f32[4,128,128]{1,2,0:T(8,128)S(1)} custom-call(f32[4,128,128]{2,1,0:T(8,128)} %get-tuple-element.386), custom_call_target="InvertDiagBlocksLowerTriangular" | custom-call | tf_op jit(solution)/shard_map/while/body/eval_jaxpr/jit(_solve_triangular)/triangular_solve | solution.py:88
  407.5 38.4 %psum.49 = f32[8,512]{1,0:T(8,128)S(1)} all-reduce(f32[8,512]{1,0:T(8,128)S(1)} %fusion.88), channel_id=1, replica_groups=mesh['gen'=4,'fit'=8] {'gen','fit'}, use_global_device_ids=true, to_apply=%region_11.11 | all-reduce | flops 4096 | bytes 32768 | tf_op jit(solution)/shard_map/while/body/eval_jaxpr/psum | solution.py:12
  457.2 40.1 %custom-call.28 = f32[4,128,128]{1,2,0:T(8,128)S(1)} custom-call(f32[4,128,128]{2,1,0:T(8,128)} %get-tuple-element.386), custom_call_target="InvertDiagBlocksLowerTriangular" | custom-call | tf_op jit(solution)/shard_map/while/body/eval_jaxpr/jit(_solve_triangular)/triangular_solve | solution.py:88
  515.5 38.4 %psum.49 = f32[8,512]{1,0:T(8,128)S(1)} all-reduce(f32[8,512]{1,0:T(8,128)S(1)} %fusion.88), channel_id=1, replica_groups=mesh['gen'=4,'fit'=8] {'gen','fit'}, use_global_device_ids=true, to_apply=%region_11.11 | all-reduce | flops 4096 | bytes 32768 | tf_op jit(solution)/shard_map/while/body/eval_jaxpr/psum | solution.py:12
  565.1 40.1 %custom-call.28 = f32[4,128,128]{1,2,0:T(8,128)S(1)} custom-call(f32[4,128,128]{2,1,0:T(8,128)} %get-tuple-element.386), custom_call_target="InvertDiagBlocksLowerTriangular" | custom-call | tf_op jit(solution)/shard_map/while/body/eval_jaxpr/jit(_solve_triangular)/triangular_solve | solution.py:88
  623.4 38.4 %psum.49 = f32[8,512]{1,0:T(8,128)S(1)} all-reduce(f32[8,512]{1,0:T(8,128)S(1)} %fusion.88), channel_id=1, replica_groups=mesh['gen'=4,'fit'=8] {'gen','fit'}, use_global_device_ids=true, to_apply=%region_11.11 | all-reduce | flops 4096 | bytes 32768 | tf_op jit(solution)/shard_map/while/body/eval_jaxpr/psum | solution.py:12
  673.1 40.1 %custom-call.28 = f32[4,128,128]{1,2,0:T(8,128)S(1)} custom-call(f32[4,128,128]{2,1,0:T(8,128)} %get-tuple-element.386), custom_call_target="InvertDiagBlocksLowerTriangular" | custom-call | tf_op jit(solution)/shard_map/while/body/eval_jaxpr/jit(_solve_triangular)/triangular_solve | solution.py:88
  731.4 38.4 %psum.49 = f32[8,512]{1,0:T(8,128)S(1)} all-reduce(f32[8,512]{1,0:T(8,128)S(1)} %fusion.88), channel_id=1, replica_groups=mesh['gen'=4,'fit'=8] {'gen','fit'}, use_global_device_ids=true, to_apply=%region_11.11 | all-reduce | flops 4096 | bytes 32768 | tf_op jit(solution)/shard_map/while/body/eval_jaxpr/psum | solution.py:12
  781.0 40.1 %custom-call.28 = f32[4,128,128]{1,2,0:T(8,128)S(1)} custom-call(f32[4,128,128]{2,1,0:T(8,128)} %get-tuple-element.386), custom_call_target="InvertDiagBlocksLowerTriangular" | custom-call | tf_op jit(solution)/shard_map/while/body/eval_jaxpr/jit(_solve_triangular)/triangular_solve | solution.py:88
  821.2 16.7 %psum.48 = f32[512,8]{0,1:T(8,128)S(1)} all-reduce(f32[512,8]{0,1:T(8,128)S(1)} %bitcast.105), channel_id=1, replica_groups=mesh['gen'=4,'fit'=8] {'gen'}, use_global_device_ids=true, to_apply=%region_10.10 | all-reduce | flops 4096 | bytes 32768 | tf_op jit(solution)/shard_map/while/body/eval_jaxpr/psum | solution.py:86
  839.4 38.4 %psum.49 = f32[8,512]{1,0:T(8,128)S(1)} all-reduce(f32[8,512]{1,0:T(8,128)S(1)} %fusion.88), channel_id=1, replica_groups=mesh['gen'=4,'fit'=8] {'gen','fit'}, use_global_device_ids=true, to_apply=%region_11.11 | all-reduce | flops 4096 | bytes 32768 | tf_op jit(solution)/shard_map/while/body/eval_jaxpr/psum | solution.py:12
  889.0 40.1 %custom-call.28 = f32[4,128,128]{1,2,0:T(8,128)S(1)} custom-call(f32[4,128,128]{2,1,0:T(8,128)} %get-tuple-element.386), custom_call_target="InvertDiagBlocksLowerTriangular" | custom-call | tf_op jit(solution)/shard_map/while/body/eval_jaxpr/jit(_solve_triangular)/triangular_solve | solution.py:88
  929.1 16.8 %psum.48 = f32[512,8]{0,1:T(8,128)S(1)} all-reduce(f32[512,8]{0,1:T(8,128)S(1)} %bitcast.105), channel_id=1, replica_groups=mesh['gen'=4,'fit'=8] {'gen'}, use_global_device_ids=true, to_apply=%region_10.10 | all-reduce | flops 4096 | bytes 32768 | tf_op jit(solution)/shard_map/while/body/eval_jaxpr/psum | solution.py:86
  947.3 38.4 %psum.49 = f32[8,512]{1,0:T(8,128)S(1)} all-reduce(f32[8,512]{1,0:T(8,128)S(1)} %fusion.88), channel_id=1, replica_groups=mesh['gen'=4,'fit'=8] {'gen','fit'}, use_global_device_ids=true, to_apply=%region_11.11 | all-reduce | flops 4096 | bytes 32768 | tf_op jit(solution)/shard_map/while/body/eval_jaxpr/psum | solution.py:12
  996.9 40.1 %custom-call.28 = f32[4,128,128]{1,2,0:T(8,128)S(1)} custom-call(f32[4,128,128]{2,1,0:T(8,128)} %get-tuple-element.386), custom_call_target="InvertDiagBlocksLowerTriangular" | custom-call | tf_op jit(solution)/shard_map/while/body/eval_jaxpr/jit(_solve_triangular)/triangular_solve | solution.py:88
  1037.1 16.8 %psum.48 = f32[512,8]{0,1:T(8,128)S(1)} all-reduce(f32[512,8]{0,1:T(8,128)S(1)} %bitcast.105), channel_id=1, replica_groups=mesh['gen'=4,'fit'=8] {'gen'}, use_global_device_ids=true, to_apply=%region_10.10 | all-reduce | flops 4096 | bytes 32768 | tf_op jit(solution)/shard_map/while/body/eval_jaxpr/psum | solution.py:86
  1055.3 38.4 %psum.49 = f32[8,512]{1,0:T(8,128)S(1)} all-reduce(f32[8,512]{1,0:T(8,128)S(1)} %fusion.88), channel_id=1, replica_groups=mesh['gen'=4,'fit'=8] {'gen','fit'}, use_global_device_ids=true, to_apply=%region_11.11 | all-reduce | flops 4096 | bytes 32768 | tf_op jit(solution)/shard_map/while/body/eval_jaxpr/psum | solution.py:12
  1104.9 40.1 %custom-call.28 = f32[4,128,128]{1,2,0:T(8,128)S(1)} custom-call(f32[4,128,128]{2,1,0:T(8,128)} %get-tuple-element.386), custom_call_target="InvertDiagBlocksLowerTriangular" | custom-call | tf_op jit(solution)/shard_map/while/body/eval_jaxpr/jit(_solve_triangular)/triangular_solve | solution.py:88
  1145.0 16.8 %psum.48 = f32[512,8]{0,1:T(8,128)S(1)} all-reduce(f32[512,8]{0,1:T(8,128)S(1)} %bitcast.105), channel_id=1, replica_groups=mesh['gen'=4,'fit'=8] {'gen'}, use_global_device_ids=true, to_apply=%region_10.10 | all-reduce | flops 4096 | bytes 32768 | tf_op jit(solution)/shard_map/while/body/eval_jaxpr/psum | solution.py:86
  1163.2 38.4 %psum.49 = f32[8,512]{1,0:T(8,128)S(1)} all-reduce(f32[8,512]{1,0:T(8,128)S(1)} %fusion.88), channel_id=1, replica_groups=mesh['gen'=4,'fit'=8] {'gen','fit'}, use_global_device_ids=true, to_apply=%region_11.11 | all-reduce | flops 4096 | bytes 32768 | tf_op jit(solution)/shard_map/while/body/eval_jaxpr/psum | solution.py:12
  (334 shorter events, 418.3 us)
Async XLA Ops:
  6.5 80.0 %copy-start.2 = (bf16[500,512]{1,0:T(8,128)(2,1)S(1)}, bf16[500,512]{1,0:T(8,128)(2,1)}, u32[]{:S(2)}) copy-start(bf16[500,512]{1,0:T(8,128)(2,1)} %param.10) | copy-start | bytes 1536004
  6.5 173.2 %all-reduce.4.cloned.1.call-start = ((), (), s32[]{:S(2)}) async-start(), calls=%async_computation | async-start | bytes 4194304 | tf_op jit(solution)/shard_map/psum | solution.py:12
  6.5 11.5 collective-permute-start
  18.1 10.3 collective-permute-start.1
  28.4 10.3 collective-permute-start.2
  38.7 10.3 collective-permute-start.3
  49.0 10.3 collective-permute-start.4
  59.4 10.4 collective-permute-start.5
  69.8 10.6 collective-permute-start.6
  86.6 3.2 copy-start.1
  93.4 245.4 %all-reduce.6.cloned.1.call-start = ((), (), s32[]{:S(2)}) async-start(), calls=%async_computation.1 | async-start | bytes 262144
  179.7 159.8 %copy-start = (f32[512,1024]{1,0:T(8,128)S(1)}, f32[512,1024]{1,0:T(8,128)}, u32[]{:S(2)}) copy-start(f32[512,1024]{1,0:T(8,128)} %param.11) | copy-start | bytes 6291460
  1202.6 0.6 copy-start.3
Sparse Core Ops, SparseCore 0:
  93.5 68.9 all-reduce.3
  215.7 123.0 all-reduce.5
